TPU v7x, 32 devices: a whole 2x2x4 slice. The times are simulated.
32 devices in a mesh: row: 8 (over y, x, core), col: 4 (over z).
Axes of the slice: x: 2, y: 2, z: 4, core: 2. Of those that a mesh axis runs over, the one named last changes fastest.
Arguments:
- features: bfloat16 [16384, 512], P(('row', 'col')), may hold values from -6 to 6
- weight: bfloat16 [512, 512], replicated, may hold values from -0.25 to 0.25
- bias: float32 [512], replicated, may hold values from -3 to 3
- cotangent: bfloat16 [16384, 512], P(('row', 'col')), may hold values from -6 to 6
- tile_values: bfloat16 [8, 4, 64, 128, 128], P('row', 'col'), may hold values from -0.1875 to 0.1875
- tile_rows: int32 [8, 4, 64], P('row', 'col'), may hold values from 0 to 127, as said below
- tile_cols: int32 [8, 4, 64], P('row', 'col'), may hold values from 0 to 127, as said below
- tile_counts: int32 [8, 4], P('row', 'col'), may hold values from 1 to 64
Outputs:
- output: bfloat16 [16384, 512], P(('row', 'col'))
- feature_grad: bfloat16 [16384, 512], P(('row', 'col'))
- weight_grad: float32 [512, 512], replicated
- bias_grad: float32 [512], replicated
Inputs may be any that keep to these rules, and one draw needn't show every extreme that they name: `tile_rows`: A tile on device (p, q) has its row block in row group p, that is row block // 16 == p, and its column block's atoms on devices of index q along col, that is (column block // 4) % 4 == q. The rows of features held by device (p, q) are blocks p * 4 * 4 + q * 4 to that plus 4 - 1. Row and column pairs may repeat. `tile_cols`: among one device's live tiles at most 16 have their row block held by any one device of that row group, and at most 8 have their column block held by any one device of that column group.
All inputs are finite; a program needn't handle non-finite values.
Results may differ from a plain program's by a relative error of at most 0.013.
Values may be sent and summed in bfloat16 or wider, within the bound.
A program may use at most 128 MiB of HBM per device.

v0:
```python
import math

import jax
import jax.numpy as jnp
from jax import lax
from jax.sharding import PartitionSpec as P


def sum_rows(products, local_ids, alive_mask, total_blocks):
    block_size = products.shape[1]
    feature_width = products.shape[2]
    target_ids = jnp.where(alive_mask, local_ids, total_blocks)
    blank_sum = jnp.zeros((total_blocks, block_size, feature_width), jnp.float32)
    summed = blank_sum.at[target_ids].add(products, mode="drop")
    return summed.reshape(total_blocks * block_size, feature_width)


def on_device(features, weight, bias, cotangent, tile_values, tile_rows, tile_cols, tile_counts):
    row_count = lax.axis_size("row")
    col_count = lax.axis_size("col")
    node_dev, feature_width = features.shape
    slot_count = tile_values.shape[2]
    block_size = tile_values.shape[3]
    blk_dev = node_dev // block_size
    atom_count = node_dev * row_count * col_count
    values = tile_values.reshape(slot_count, block_size, block_size)
    alive_mask = jnp.arange(slot_count) < tile_counts.reshape(())
    row_local = tile_rows.reshape(slot_count) % (blk_dev * col_count)
    col_ids = tile_cols.reshape(slot_count)
    col_local = col_ids // (blk_dev * col_count) * blk_dev + col_ids % blk_dev
    gathered = lax.all_gather(features, "row", axis=0, tiled=True).reshape(
        row_count * blk_dev, block_size, feature_width
    )
    sources = gathered[col_local]
    products = jnp.einsum("kab,kbd->kad", values, sources, preferred_element_type=jnp.float32)
    partial_value = sum_rows(products, row_local, alive_mask, blk_dev * col_count)
    summed = lax.psum_scatter(partial_value, "col", scatter_dimension=0, tiled=True)
    aggregated = summed.astype(jnp.bfloat16)
    pre_act = jnp.dot(aggregated, weight, preferred_element_type=jnp.float32) + bias
    sigm = jax.nn.sigmoid(pre_act)
    output = (pre_act * sigm).astype(jnp.bfloat16)
    grad_pre = (cotangent.astype(jnp.float32) * sigm * (1.0 + pre_act * (1.0 - sigm))).astype(
        jnp.bfloat16
    )
    scale = 1.0 / math.sqrt(atom_count)
    weight_part = jnp.dot(aggregated.T, grad_pre, preferred_element_type=jnp.float32) * scale
    bias_part = jnp.sum(grad_pre.astype(jnp.float32), axis=0) * scale
    weight_grad, bias_grad = lax.psum((weight_part, bias_part), ("row", "col"))
    grad_agg = jnp.dot(grad_pre, weight.T, preferred_element_type=jnp.float32).astype(jnp.bfloat16)
    spread = lax.all_gather(grad_agg, "col", axis=0, tiled=True).reshape(
        col_count * blk_dev, block_size, feature_width
    )
    upstream = spread[row_local]
    back_products = jnp.einsum("kba,kbd->kad", values, upstream, preferred_element_type=jnp.float32)
    grad_partial = sum_rows(back_products, col_local, alive_mask, blk_dev * row_count)
    grad_summed = lax.psum_scatter(
        grad_partial.astype(jnp.bfloat16), "row", scatter_dimension=0, tiled=True
    )
    return (output, grad_summed, weight_grad, bias_grad)


def solution(mesh):
    return jax.shard_map(
        on_device,
        mesh=mesh,
        in_specs=(
            P(("row", "col"), None),
            P(),
            P(),
            P(("row", "col"), None),
            P("row", "col", None, None, None),
            P("row", "col", None),
            P("row", "col", None),
            P("row", "col"),
        ),
        out_specs=(P(("row", "col"), None), P(("row", "col"), None), P(), P()),
        check_vma=False,
    )
```

profile of v0, /device:TPU:1, one launch (start us, length us, event | category | flops | bytes accessed | tf_op | source)
XLA Modules:
  0.0 447.2 jit_solution(17194235437523508426)
XLA Ops:
  7.2 0.0 all-gather.3.cloned.1.call-start
  7.2 0.7 all-gather.3.cloned.1.call-update
  7.9 0.0 reduce-scatter.3.cloned.1.call-start
  8.6 0.7 fusion.8
  9.3 0.7 fusion.9
  10.0 39.0 %all-gather.3.cloned.1.call-done = bf16[4096,512]{1,0:T(8,128)(2,1)} async-done(((bf16[512,512]{1,0:T(8,128)(2,1)}), bf16[4096,512]{1,0:T(8,128)(2,1)}) %all-gather.3.cloned.1.call-update) | async-done | bytes 4194320 | tf_op jit(solution)/shard_map/all_gather | solution.py:31
  49.0 7.7 %gather_fusion = bf16[64,128,512]{2,1,0:T(8,128)(2,1)} fusion(bf16[32,128,512]{2,1,0:T(8,128)(2,1)} %bitcast.47, s32[1024]{0:T(1024)S(1)} %pad_clamp_fusion.1), kind=kCustom, calls=%fused_computation | custom fusion | bytes 16777472 | tf_op jit(solution)/shard_map/gather | solution.py:34
  56.7 11.5 %convolution_bitcast_fusion.1 = f32[64,128,512]{1,2,0:T(8,128)} fusion(bf16[64,128,512]{2,1,0:T(8,128)(2,1)} %gather_fusion, bf16[1,1,64,128,128]{4,3,2,1,0:T(8,128)(2,1)S(1)} %copy-done), kind=kOutput, calls=%fused_computation.5 | convolution fusion | flops 1073741824 | bytes 27262976 | tf_op jit(solution)/shard_map/kab,kbd->kad/dot_general | solution.py:35
  68.2 17.5 %copy.15 = f32[64,128,512]{2,1,0:T(8,128)} copy(f32[64,128,512]{1,2,0:T(8,128)} %convolution_bitcast_fusion.1) | data formatting | bytes 33554432 | tf_op jit(solution)/shard_map/kab,kbd->kad/dot_general | solution.py:35
  85.6 2.5 broadcast_in_dim.7
  88.1 32.8 %scatter_fusion = f32[16,128,512]{2,1,0:T(8,128)} fusion(f32[16,128,512]{2,1,0:T(8,128)} %broadcast_in_dim.7, s32[64]{0:T(128)S(1)} %fusion.6, f32[64,128,512]{2,1,0:T(8,128)} %copy.15), kind=kCustom, calls=%fused_computation.2 | custom fusion | flops 4194304 | bytes 50331904 | tf_op jit(solution)/shard_map/scatter-add | solution.py:14
  120.9 0.0 reduce-scatter.3.cloned.1.call-update
  121.0 0.0 all-gather.5.cloned.1.call-start
  121.0 77.6 %reduce-scatter.3.cloned.1.call-done = f32[512,512]{1,0:T(8,128)} async-done(((f32[2048,512]{1,0:T(8,128)}), f32[512,512]{1,0:T(8,128)}) %reduce-scatter.3.cloned.1.call-update) | async-done | bytes 1048592 | tf_op jit(solution)/shard_map/reduce_scatter | solution.py:37
  198.6 3.0 convert_reduce_fusion
  201.6 1.3 convolution_convert_fusion
  202.9 0.0 all-gather.5.cloned.1.call-update
  202.9 0.0 all-reduce.2.cloned.1.call-start
  203.0 2.7 convolution_multiply_fusion
  205.7 0.0 all-reduce.2.cloned.1.call-update
  205.7 0.2 reduce-scatter.5.cloned.1.call-start
  205.9 43.5 %all-gather.5.cloned.1.call-done = bf16[2048,512]{1,0:T(8,128)(2,1)} async-done(((bf16[512,512]{1,0:T(8,128)(2,1)}), bf16[2048,512]{1,0:T(8,128)(2,1)}) %all-gather.5.cloned.1.call-update) | async-done | bytes 2097168 | tf_op jit(solution)/shard_map/all_gather | solution.py:50
  249.4 7.1 %gather_fusion.1 = bf16[64,128,512]{2,1,0:T(8,128)(2,1)} fusion(bf16[16,128,512]{2,1,0:T(8,128)(2,1)} %bitcast.46, s32[1024]{0:T(1024)S(1)} %pad_clamp_fusion), kind=kCustom, calls=%fused_computation.1 | custom fusion | bytes 16777472 | tf_op jit(solution)/shard_map/gather | solution.py:53
  256.5 11.5 %convolution_bitcast_fusion = f32[64,128,512]{1,2,0:T(8,128)} fusion(bf16[64,128,512]{2,1,0:T(8,128)(2,1)} %gather_fusion.1, bf16[1,1,64,128,128]{4,3,2,1,0:T(8,128)(2,1)S(1)} %copy-done), kind=kOutput, calls=%fused_computation.4 | convolution fusion | flops 1073741824 | bytes 27262976 | tf_op jit(solution)/shard_map/kba,kbd->kad/dot_general | solution.py:54
  267.9 17.5 %copy.17 = f32[64,128,512]{2,1,0:T(8,128)} copy(f32[64,128,512]{1,2,0:T(8,128)} %convolution_bitcast_fusion) | data formatting | bytes 33554432 | tf_op jit(solution)/shard_map/kba,kbd->kad/dot_general | solution.py:54
  285.5 4.3 broadcast_in_dim.8
  289.8 32.8 %scatter_fusion.1 = f32[32,128,512]{2,1,0:T(8,128)} fusion(f32[32,128,512]{2,1,0:T(8,128)} %broadcast_in_dim.8, s32[64]{0:T(128)S(1)} %get-tuple-element.8, f32[64,128,512]{2,1,0:T(8,128)} %copy.17), kind=kCustom, calls=%fused_computation.3 | custom fusion | flops 4194304 | bytes 50331904 | tf_op jit(solution)/shard_map/scatter-add | solution.py:14
  322.6 6.0 %convert_element_type.29 = bf16[32,128,512]{2,1,0:T(8,128)(2,1)} convert(f32[32,128,512]{2,1,0:T(8,128)} %scatter_fusion.1) | non-fusion elementwise | flops 2097152 | bytes 12582912 | tf_op jit(solution)/shard_map/convert_element_type | solution.py:57
  328.6 41.5 %psum.15 = f32[512]{0:T(512)} all-reduce(f32[512]{0:T(512)S(1)} %broadcast_multiply_fusion), channel_id=1, replica_groups=mesh['row'=8,'col'=4] {'row','col'}, use_global_device_ids=true, to_apply=%region_6.7 | all-reduce | flops 512 | bytes 4096 | tf_op jit(solution)/shard_map/psum | solution.py:48
  370.1 13.7 %all-reduce.2.cloned.1.call-done = f32[512,512]{1,0:T(8,128)} async-done(((f32[512,512]{1,0:T(8,128)}), f32[512,512]{1,0:T(8,128)}) %all-reduce.2.cloned.1.call-update) | async-done | bytes 1048592 | tf_op jit(solution)/shard_map/psum | solution.py:48
  383.8 54.6 %reduce-scatter.5.cloned.1.call-done = bf16[512,512]{1,0:T(8,128)(2,1)} async-done(((bf16[4096,512]{1,0:T(8,128)(2,1)}), bf16[512,512]{1,0:T(8,128)(2,1)}) %reduce-scatter.5.cloned.1.call-update) | async-done | bytes 524304 | tf_op jit(solution)/shard_map/reduce_scatter | solution.py:56
  438.4 2.3 copy.24
  (12 shorter events, 0.1 us)
Async XLA Ops:
  7.2 49.5 %copy-start = (bf16[1,1,64,128,128]{4,3,2,1,0:T(8,128)(2,1)S(1)}, bf16[1,1,64,128,128]{4,3,2,1,0:T(8,128)(2,1)}, u32[]{:S(2)}) copy-start(bf16[1,1,64,128,128]{4,3,2,1,0:T(8,128)(2,1)} %param.12) | copy-start | bytes 6291460
  7.2 41.8 %all-gather.3.cloned.1.call-start = ((), (), s32[]{:S(2)}) async-start(), calls=%async_computation.2 | async-start | bytes 4718592 | tf_op jit(solution)/shard_map/all_gather | solution.py:31
  7.9 190.7 %reduce-scatter.3.cloned.1.call-start = ((), (), s32[]{:S(2)}) async-start(), calls=%async_computation.3 | async-start | bytes 5242880 | tf_op jit(solution)/shard_map/reduce_scatter | solution.py:37
  88.1 110.5 %copy-start.1 = (bf16[512,512]{1,0:T(8,128)(2,1)S(1)}, bf16[512,512]{1,0:T(8,128)(2,1)}, u32[]{:S(2)}) copy-start(bf16[512,512]{1,0:T(8,128)(2,1)} %param.9) | copy-start | bytes 1572868
  88.1 110.5 %copy-start.2 = (f32[512]{0:T(512)S(1)}, f32[512]{0:T(512)}, u32[]{:S(2)}) copy-start(f32[512]{0:T(512)} %param.10) | copy-start | bytes 6148
  121.0 128.4 %all-gather.5.cloned.1.call-start = ((), (), s32[]{:S(2)}) async-start(), calls=%async_computation.4 | async-start | bytes 2621440 | tf_op jit(solution)/shard_map/all_gather | solution.py:50
  202.9 180.9 %all-reduce.2.cloned.1.call-start = ((), (), s32[]{:S(2)}) async-start(), calls=%async_computation.6 | async-start | bytes 2097152 | tf_op jit(solution)/shard_map/psum | solution.py:48
  205.7 232.7 %reduce-scatter.5.cloned.1.call-start = ((), (), s32[]{:S(2)}) async-start(), calls=%async_computation.5 | async-start | bytes 4718592 | tf_op jit(solution)/shard_map/reduce_scatter | solution.py:56
Sparse Core Ops, SparseCore 0:
  9.9 39.0 all-gather.2
  121.1 77.4 reduce-scatter.2
  203.1 46.2 all-gather.4
  255.0 128.7 all-reduce.1
  387.6 50.7 reduce-scatter.4
where the time goes:
time: 449 us; the launch traced here: 447 us
  waiting for transfers between devices  229 us (51%)
  other arithmetic  73 us (16%)
  local copies, waits for them, and re-layouts  58.8 us (13%)
  blocking collectives  41.5 us (9%)
  matrix products  29.9 us (7%)
  between operations  14.5 us (3%)
    reduce_scatter x1, waiting for transfers between devices, on_device(): lax.psum_scatter(partial_value, 'col', scatter_dimension=0, tiled=True)  77.6 us
    scatter-add x2, other arithmetic, sum_rows(): summed = blank_sum.at[target_ids].add(products, mode='drop')  65.6 us
    reduce_scatter x1, waiting for transfers between devices, on_device(): lax.psum_scatter(grad_partial.astype(jnp.bfloat16), 'row', scatter_dimens...  54.6 us
    all_gather x1, waiting for transfers between devices, on_device(): lax.all_gather(grad_agg, 'col', axis=0, tiled=True)  43.5 us
    psum x1, blocking collectives, on_device(): weight_grad, bias_grad = lax.psum((weight_part, bias_part), ('row', 'col'))  41.5 us
    all_gather x1, waiting for transfers between devices, on_device(): lax.all_gather(features, 'row', axis=0, tiled=True)  39 us
    dot_general x1, local copies, waits for them, and re-layouts, on_device(): jnp.einsum('kba,kbd->kad', values, upstream, preferred_element_type=jnp.f...  17.5 us
    dot_general x1, local copies, waits for them, and re-layouts, on_device(): jnp.einsum('kab,kbd->kad', values, sources, preferred_element_type=jnp.fl...  17.5 us
  transfers between devices with their start and end apart: 5, of which 5 were waited for; matrix products, arithmetic and copies ran while one was open for 19% of the time, Pallas kernels for 0%

commit v1 on v0

v1 whole, which is shorter than its diff:
```python
import functools
import math

import jax
import jax.numpy as jnp
from jax import lax
from jax.experimental import pallas as pl
from jax.experimental.pallas import tpu as pltpu
from jax.sharding import PartitionSpec as P

MESH = pl.DeviceIdType.MESH
BF = jnp.bfloat16
F32 = jnp.float32
PAD = 16


def flip(k, bits):
    out = k
    for b in range(8):
        step = 1 << b
        if bits & step:
            out = out + step - 2 * step * ((k // step) % 2)
    return out


def remote(src, dst, send, recv, to):
    return pltpu.make_async_remote_copy(
        src_ref=src, dst_ref=dst, send_sem=send, recv_sem=recv, device_id=to, device_id_type=MESH
    )


def greet(peers):
    barrier = pltpu.get_barrier_semaphore()
    for peer in peers:
        pl.semaphore_signal(barrier, inc=1, device_id=peer, device_id_type=MESH)
    pl.semaphore_wait(barrier, len(peers))


def gather_kernel(chips, nb, feats, out, held, own_sem, s_same, r_same, s_part, r_part):
    r, q = lax.axis_index("row"), lax.axis_index("col")
    k, c = r // 2, r % 2
    hb = nb // 2
    relay = chips == 4
    near = [d for d in range(1, chips) if not (relay and d == 3)]
    partner = (k * 2 + 1 - c, q)

    def dev(d):
        return (flip(k, d) * 2 + c, q)

    def slot(d, core, h):
        return out.at[pl.ds((flip(k, d) * 2 + core) * nb + h * hb, hb)]

    def own(d, h):
        return remote(
            feats.at[pl.ds(h * hb, hb)], slot(0, c, h), s_same.at[d, h], r_same.at[d, h], dev(d)
        )

    def pass_on(h):
        via, to = (1, 2) if h == 0 else (2, 1)
        return remote(slot(via, c, h), slot(via, c, h), s_same.at[3, h], r_same.at[3, h], dev(to))

    def inc(d, h):
        return remote(slot(d, c, h), slot(d, c, h), s_same.at[d, h], r_same.at[d, h], dev(d))

    def fwd(d, h):
        src = feats.at[pl.ds(h * hb, hb)] if d == 0 else slot(d, c, h)
        return remote(src, slot(d, c, h), s_part.at[d, h], r_part.at[d, h], partner)

    def inc_part(d, h):
        return remote(
            slot(d, 1 - c, h), slot(d, 1 - c, h), s_part.at[d, h], r_part.at[d, h], partner
        )

    greet([partner] + [dev(d) for d in near])
    take = pltpu.make_async_copy(feats, held, own_sem.at[0])
    take.start()
    for n in range(2):
        for d in near:
            own(d, (n + (d == 2)) % 2).start()
    for h in range(2):
        fwd(0, h).start()
    take.wait()
    put = pltpu.make_async_copy(held, out.at[pl.ds(r * nb, nb)], own_sem.at[1])
    put.start()
    for n in range(2):
        for d in near:
            h = (n + (d == 2)) % 2
            inc(d, h).wait_recv()
            if relay and n == 0:
                pass_on(h).start()
            fwd(d, h).start()
    if relay:
        for h in range(2):
            inc(3, h).wait_recv()
            fwd(3, h).start()
    for d in range(chips):
        for h in range(2):
            inc_part(d, h).wait_recv()
    for h in range(2):
        for d in near:
            own(d, h).wait_send()
        if relay:
            pass_on(h).wait_send()
        for d in range(chips):
            fwd(d, h).wait_send()
    put.wait()


def tile_kernel(
    back, group, blk, ncol, counts, rows, cols, tiles, src, out, lists, lens, acc
):
    slots, size = tiles.shape[0], tiles.shape[1]
    dests = out.shape[0]
    span = blk * ncol

    def row_id(k):
        return rows[k] % span

    def col_id(k):
        g = cols[k]
        return g // span * blk + g % blk

    dst_of, src_of = (col_id, row_id) if back else (row_id, col_id)

    @pl.loop(0, dests)
    def _(d):
        lens[d] = 0

    @pl.loop(0, counts[0])
    def _(k):
        d = dst_of(k)
        n = lens[d]
        lists[d * slots + n] = k
        lens[d] = n + 1

    @pl.loop(0, dests)
    def _(d):
        m = lens[d]
        acc[...] = jnp.zeros_like(acc)

        @pl.loop(0, (m + group - 1) // group)
        def _(t):
            left, right = [], []
            for i in range(group):
                at = t * group + i
                k = lists[d * slots + jnp.minimum(at, m - 1)]
                mat = tiles[k]
                left.append(jnp.where(at < m, mat, jnp.zeros_like(mat)))
                right.append(src[src_of(k)])
            lhs = jnp.concatenate(left, axis=0 if back else 1)
            rhs = jnp.concatenate(right, axis=0)
            dims = (((0,), (0,)), ((), ())) if back else (((1,), (0,)), ((), ()))
            acc[...] += lax.dot_general(lhs, rhs, dims, preferred_element_type=F32)

        out[d] = acc[...].astype(BF)


def middle_kernel(
    n, nb, scale, part, w, bias, cot, out, spread, wp,
    acc_r, acc_l, agg, gp, accf, s_r, r_r, s_l, r_l, s_gr, r_gr, s_gl, r_gl,
):
    r, q = lax.axis_index("row"), lax.axis_index("col")
    last = n - 1
    right, left = (r, jnp.minimum(q + 1, last)), (r, jnp.maximum(q - 1, 0))
    size = part.shape[1]

    def chain(buf, s, v, to, d, j, first=False):
        at = d * nb + j
        return remote(
            (part if first else buf).at[at], buf.at[at], s.at[d, j], v.at[d, j], to
        )

    cp_r = functools.partial(chain, acc_r, s_r, r_r, right)
    cp_l = functools.partial(chain, acc_l, s_l, r_l, left)

    def cp_g(s, v, to, d, j):
        at = d * nb + j
        return remote(spread.at[at], spread.at[at], s.at[d, j], v.at[d, j], to)

    cp_gr = functools.partial(cp_g, s_gr, r_gr, right)
    cp_gl = functools.partial(cp_g, s_gl, r_gl, left)

    def hop(cp, buf, mine, start, d, j):
        @pl.when(mine)
        def _():
            @pl.when(start)
            def _():
                cp(d, j, True).start()

            @pl.when(jnp.logical_not(start))
            def _():
                cp(d, j).wait_recv()
                at = d * nb + j
                buf[at] = (buf[at].astype(F32) + part[at].astype(F32)).astype(BF)
                cp(d, j).start()

    def reduce_block(j):
        for i in range(n - 1):
            hop(cp_r, acc_r, q < last - i, q == 0, last - i, j)
            hop(cp_l, acc_l, q > i, q == last, i, j)

    def finish_block(j):
        at = q * nb + j
        accf[...] = part[at].astype(F32)

        @pl.when(q > 0)
        def _():
            cp_r(q, j).wait_recv()
            accf[...] += acc_r[at].astype(F32)

        @pl.when(q < last)
        def _():
            cp_l(q, j).wait_recv()
            accf[...] += acc_l[at].astype(F32)

        rows = pl.ds(j * size, size)
        a = accf[...].astype(BF)
        agg[rows, :] = a
        pre = jnp.dot(a, w[...], preferred_element_type=F32) + bias[...]
        sig = jax.nn.sigmoid(pre)
        out[rows, :] = (pre * sig).astype(BF)
        g = (cot[rows, :].astype(F32) * sig * (1.0 + pre * (1.0 - sig))).astype(BF)
        gp[rows, :] = g
        spread[at] = lax.dot_general(
            g, w[...], (((1,), (1,)), ((), ())), preferred_element_type=F32
        ).astype(BF)

        @pl.when(q < last)
        def _():
            cp_gr(q, j).start()

        @pl.when(q > 0)
        def _():
            cp_gl(q, j).start()

    def relay_block(j):
        for o in range(1, n):
            @pl.when(q >= o)
            def _():
                cp_gr(q - o, j).wait_recv()

                @pl.when(q < last)
                def _():
                    cp_gr(q - o, j).start()

            @pl.when(q + o <= last)
            def _():
                cp_gl(q + o, j).wait_recv()

                @pl.when(q > 0)
                def _():
                    cp_gl(q + o, j).start()

    barrier = pltpu.get_barrier_semaphore()

    @pl.when(q > 0)
    def _():
        pl.semaphore_signal(barrier, inc=1, device_id=left, device_id_type=MESH)

    @pl.when(q < last)
    def _():
        pl.semaphore_signal(barrier, inc=1, device_id=right, device_id_type=MESH)

    pl.semaphore_wait(barrier, jnp.minimum(q, 1) + jnp.minimum(last - q, 1))

    for step in range(nb + 3):
        if step < nb:
            reduce_block(step)
        if 0 <= step - 1 < nb:
            finish_block(step - 1)
        if 0 <= step - 3 < nb:
            if step == nb + 2:
                weight_block(n, scale, agg, gp, wp)
            relay_block(step - 3)

    for j in range(nb):
        for d in range(n):
            @pl.when(q < d)
            def _():
                cp_r(d, j).wait_send()

            @pl.when(q > d)
            def _():
                cp_l(d, j).wait_send()

            @pl.when(jnp.logical_and(q >= d, q < last))
            def _():
                cp_gr(d, j).wait_send()

            @pl.when(jnp.logical_and(q <= d, q > 0))
            def _():
                cp_gl(d, j).wait_send()


def weight_block(n, scale, agg, gp, wp):
    width = agg.shape[1]
    rows = width // (2 * n)
    total = jnp.sum(gp[...].astype(F32), axis=0, keepdims=True) * scale
    pad = jnp.broadcast_to(total, (PAD, width)).astype(BF)
    step = 128
    for t in range(width // step):
        res = lax.dot_general(
            agg[:, t * step : (t + 1) * step],
            gp[...],
            (((0,), (0,)), ((), ())),
            preferred_element_type=F32,
        )
        res = (res * scale).astype(BF)
        for u in range(step // rows):
            p = (t * step) // rows + u
            wp[p // n, p % n, :rows, :] = res[u * rows : (u + 1) * rows]
            wp[p // n, p % n, rows:, :] = pad


def add_rows(dst, srcs, begin, count):
    step = 64

    @pl.loop(0, count // step)
    def _(i):
        at = pl.ds(pl.multiple_of(begin + i * step, step), step)
        total = srcs[0][at, :].astype(F32)
        for s in srcs[1:]:
            total = total + s[at, :].astype(F32)
        dst[at, :] = total.astype(dst.dtype)


def final_kernel(
    chips, n, part, wp, fg, wg, bg, a_buf, b_buf, c_buf, w1, w2, w3, w4,
    s_a, r_a, s_b, r_b, s_c, r_c, s_w1, r_w1, s_w2, r_w2, s_w3, r_w3, s_w4, r_w4, s_w5, r_w5,
):
    r, q = lax.axis_index("row"), lax.axis_index("col")
    k, c = r // 2, r % 2
    relay = chips == 4
    near = [d for d in range(1, chips) if not (relay and d == 3)]
    partner = (k * 2 + 1 - c, q)
    rows = part.shape[1]
    half = rows // 2

    def dev(d):
        return (flip(k, d) * 2 + c, q)

    def deep(dz):
        return (r, (q + dz) % n)

    def mine(d):
        return part.at[flip(k, d) * 2 + c]

    def cp_a(d):
        return remote(
            part.at[flip(k, d) * 2 + 1 - c], a_buf.at[d], s_a.at[d], r_a.at[d], partner
        )

    def cp_b(d, h):
        at = pl.ds(h * half, half)
        return remote(a_buf.at[d, at], b_buf.at[d, at], s_b.at[d, h], r_b.at[d, h], dev(d))

    def cp_c(h):
        return remote(
            a_buf.at[3, pl.ds(h * half, half)], c_buf.at[h], s_c.at[h], r_c.at[h], dev(h + 1)
        )

    cp_w1 = remote(wp.at[1 - c], w1, s_w1.at[0], r_w1.at[0], partner)

    def cp_w2(dz):
        return remote(w1.at[(q + dz) % n], w2.at[dz], s_w2.at[dz], r_w2.at[dz], deep(dz))

    def cp_w3(d):
        return remote(w3.at[k], w3.at[k], s_w3.at[d], r_w3.at[d], dev(d))

    def cp_w4(dz):
        return remote(w4.at[c, q], w4.at[c, q], s_w4.at[dz], r_w4.at[dz], deep(dz))

    def cp_w5(dz):
        at = (q + n - dz) % n
        return remote(w4.at[c, at], w4.at[c, at], s_w5.at[dz], r_w5.at[dz], partner)

    greet([partner] + [dev(d) for d in range(1, chips)] + [deep(dz) for dz in range(1, n)])
    cp_w1.start()
    order = list(range(chips - 1, 0, -1)) + [0]
    if relay:
        order = [3, 1, 2, 0]
    for d in order:
        cp_a(d).start()

    def join(d):
        cp_a(d).wait_recv()
        add_rows(a_buf.at[d], [a_buf.at[d], mine(d)], 0, rows)

    if relay:
        join(3)
        cp_c(0).start()
        cp_c(1).start()
        join(1)
        cp_b(1, 0).start()
        join(2)
        cp_b(2, 1).start()
    else:
        for d in order[:-1]:
            join(d)
            for h in range(2):
                cp_b(d, h).start()

    cp_w1.wait_recv()
    for z in range(n):
        w1[z] = (w1[z].astype(F32) + wp[c, z].astype(F32)).astype(BF)
    for dz in range(1, n):
        cp_w2(dz).start()

    if relay:
        cp_c(0).wait_recv()
        add_rows(a_buf.at[2], [a_buf.at[2], c_buf.at[0]], 0, half)
        cp_b(2, 0).start()
        cp_c(1).wait_recv()

        @pl.loop(0, half // 64)
        def _(i):
            at = pl.ds(pl.multiple_of(half + i * 64, 64), 64)
            lo = pl.ds(pl.multiple_of(i * 64, 64), 64)
            a_buf[1, at, :] = (
                a_buf[1, at, :].astype(F32) + c_buf[1, lo, :].astype(F32)
            ).astype(BF)

        cp_b(1, 1).start()

    total = w1[q].astype(F32)
    for dz in range(1, n):
        cp_w2(dz).wait_recv()
        total = total + w2[dz].astype(F32)
    w3[k] = total.astype(BF)
    for d in range(1, chips):
        cp_w3(d).start()
    cp_a(0).wait_recv()
    for d in range(1, chips):
        other = flip(k, d)
        remote(w3.at[other], w3.at[other], s_w3.at[d], r_w3.at[d], dev(d)).wait_recv()
    total = w3[0].astype(F32)
    for i in range(1, chips):
        total = total + w3[i].astype(F32)
    w4[c, q] = total.astype(BF)
    for dz in range(1, n):
        cp_w4(dz).start()
    cp_w5(0).start()
    for dz in range(1, n):
        at = (q + n - dz) % n
        remote(
            w4.at[c, at], w4.at[c, at], s_w4.at[dz], r_w4.at[dz], deep(dz)
        ).wait_recv()
        cp_w5(dz).start()

    for d in near:
        for h in range(2):
            cp_b(d, h).wait_recv()
    add_rows(fg, [a_buf.at[0], mine(0)] + [b_buf.at[d] for d in near], 0, rows)

    for dz in range(n):
        at = (q + n - dz) % n
        remote(
            w4.at[1 - c, at], w4.at[1 - c, at], s_w5.at[dz], r_w5.at[dz], partner
        ).wait_recv()
    take = w4.shape[2] - PAD
    for i in range(2):
        for z in range(n):
            p = i * n + z
            wg[p * take : (p + 1) * take, :] = w4[i, z, :take, :].astype(F32)
    bg[...] = w4[0, 0, take:, :].astype(F32)[:8]

    cp_w1.wait_send()
    for d in range(chips):
        cp_a(d).wait_send()
    for d in near:
        for h in range(2):
            cp_b(d, h).wait_send()
    if relay:
        for h in range(2):
            cp_c(h).wait_send()
    for d in range(1, chips):
        cp_w3(d).wait_send()
    for dz in range(n):
        if dz:
            cp_w2(dz).wait_send()
            cp_w4(dz).wait_send()
        cp_w5(dz).wait_send()


VM = pl.BlockSpec(memory_space=pltpu.VMEM)
SM = pl.BlockSpec(memory_space=pltpu.SMEM)
ANY = pl.BlockSpec(memory_space=pl.ANY)


def params(cid):
    return pltpu.CompilerParams(collective_id=cid, has_side_effects=True)


def dma(*shape):
    return pltpu.SemaphoreType.DMA(shape)


def run_tiles(back, group, blk, ncol, dests, counts, rows, cols, values, src):
    slots, size = values.shape[0], values.shape[1]
    width = src.shape[2]
    return pl.pallas_call(
        functools.partial(tile_kernel, back, group, blk, ncol),
        out_shape=jax.ShapeDtypeStruct((dests, size, width), BF),
        in_specs=[SM, SM, SM, VM, VM],
        out_specs=VM,
        scratch_shapes=[
            pltpu.SMEM((dests * slots,), jnp.int32),
            pltpu.SMEM((dests,), jnp.int32),
            pltpu.VMEM((size, width), F32),
        ],
        name="tiles_back" if back else "tiles_fwd",
    )(counts, rows, cols, values, src)


def on_device(features, weight, bias, cotangent, tile_values, tile_rows, tile_cols, tile_counts):
    nrow = lax.axis_size("row")
    ncol = lax.axis_size("col")
    node_dev, width = features.shape
    slots, size = tile_values.shape[2], tile_values.shape[3]
    nb = node_dev // size
    chips = nrow // 2
    scale = 1.0 / math.sqrt(node_dev * nrow * ncol)
    values = tile_values.reshape(slots, size, size)
    rows, cols = tile_rows.reshape(slots), tile_cols.reshape(slots)
    counts = tile_counts.reshape(1)

    gathered = pl.pallas_call(
        functools.partial(gather_kernel, chips, nb),
        out_shape=jax.ShapeDtypeStruct((nrow * nb, size, width), BF),
        in_specs=[ANY],
        out_specs=ANY,
        scratch_shapes=[pltpu.VMEM((nb, size, width), BF), dma(2)] + [dma(chips, 2)] * 4,
        compiler_params=params(0),
        name="gather",
    )(features.reshape(nb, size, width))

    partial = run_tiles(False, 4, nb, ncol, ncol * nb, counts, rows, cols, values, gathered)

    pr = width // (2 * ncol) + PAD
    out, spread, wp = pl.pallas_call(
        functools.partial(middle_kernel, ncol, nb, scale),
        out_shape=[
            jax.ShapeDtypeStruct((node_dev, width), BF),
            jax.ShapeDtypeStruct((ncol * nb, size, width), BF),
            jax.ShapeDtypeStruct((2, ncol, pr, width), BF),
        ],
        in_specs=[VM] * 4,
        out_specs=[VM] * 3,
        scratch_shapes=[
            pltpu.VMEM((ncol * nb, size, width), BF),
            pltpu.VMEM((ncol * nb, size, width), BF),
            pltpu.VMEM((node_dev, width), BF),
            pltpu.VMEM((node_dev, width), BF),
            pltpu.VMEM((size, width), F32),
        ]
        + [dma(ncol, nb)] * 8,
        compiler_params=params(1),
        name="middle",
    )(partial, weight, bias.reshape(1, width), cotangent)

    grads = run_tiles(True, 2, nb, ncol, nrow * nb, counts, rows, cols, values, spread)

    fg, wg, bg = pl.pallas_call(
        functools.partial(final_kernel, chips, ncol),
        out_shape=[
            jax.ShapeDtypeStruct((node_dev, width), BF),
            jax.ShapeDtypeStruct((width, width), F32),
            jax.ShapeDtypeStruct((8, width), F32),
        ],
        in_specs=[VM] * 2,
        out_specs=[VM] * 3,
        scratch_shapes=[
            pltpu.VMEM((chips, node_dev, width), BF),
            pltpu.VMEM((chips, node_dev, width), BF),
            pltpu.VMEM((2, node_dev // 2, width), BF),
            pltpu.VMEM((ncol, pr, width), BF),
            pltpu.VMEM((ncol, pr, width), BF),
            pltpu.VMEM((chips, pr, width), BF),
            pltpu.VMEM((2, ncol, pr, width), BF),
            dma(chips), dma(chips), dma(chips, 2), dma(chips, 2), dma(2), dma(2),
            dma(1), dma(1), dma(ncol), dma(ncol), dma(chips), dma(chips),
            dma(ncol), dma(ncol), dma(ncol), dma(ncol),
        ],
        compiler_params=params(2),
        name="final",
    )(grads.reshape(nrow, node_dev, width), wp)
    return (out, fg, wg, bg[0])


def solution(mesh):
    return jax.shard_map(
        on_device,
        mesh=mesh,
        in_specs=(
            P(("row", "col"), None),
            P(),
            P(),
            P(("row", "col"), None),
            P("row", "col", None, None, None),
            P("row", "col", None),
            P("row", "col", None),
            P("row", "col"),
        ),
        out_specs=(P(("row", "col"), None), P(("row", "col"), None), P(), P()),
        check_vma=False,
    )
```

time: 449 us -> 173 us (0.39)
  waiting for transfers between devices: 229 us -> 0 us
  Pallas kernels: 0 us -> 167 us
  other arithmetic: 73 us -> 0 us
  local copies, waits for them, and re-layouts: 58.8 us -> 5.02 us
  blocking collectives: 41.5 us -> 0 us
  matrix products: 29.9 us -> 0 us
  between operations: 14.5 us -> 1.31 us
    pallas_call x0 -> x5, Pallas kernels: none -> 167 us  [the longest x1 77 us: on_device(): pl.pallas_call(functools.partial(middle_kernel, ncol, nb, scale), out_sha...]
    reduce_scatter x2 -> x0, waiting for transfers between devices: 132 us -> none  [the longest x1 77.6 us: on_device(): lax.psum_scatter(partial_value, 'col', scatter_dimension=0, tiled=True)]
    all_gather x2 -> x0, waiting for transfers between devices: 82.5 us -> none  [the longest x1 43.5 us: on_device(): lax.all_gather(grad_agg, 'col', axis=0, tiled=True)]
    scatter-add x2 -> x0, other arithmetic: 65.6 us -> none  [sum_rows(): summed = blank_sum.at[target_ids].add(products, mode='drop')]
    psum x1 -> x0, blocking collectives: 41.5 us -> none  [on_device(): weight_grad, bias_grad = lax.psum((weight_part, bias_part), ('row', 'col'))]
    dot_general x2 -> x0, local copies, waits for them, and re-layouts: 35 us -> none  [the longest x1 17.5 us: on_device(): jnp.einsum('kba,kbd->kad', values, upstream, preferred_element_type=jnp.f...]
    dot_general x5 -> x0, matrix products: 29.9 us -> none  [the longest x1 11.5 us: on_device(): jnp.einsum('kba,kbd->kad', values, upstream, preferred_element_type=jnp.f...]
    gather x2 -> x0, local copies, waits for them, and re-layouts: 14.8 us -> none  [the longest x1 7.71 us: on_device(): sources = gathered[col_local]]
  transfers between devices with their start and end apart: 5 -> 0, of which waited for: 5 -> 0; matrix products, arithmetic and copies ran while one was open for 19% -> 0% of each run, Pallas kernels for 0% -> 0%
where the time goes in v1:
time: 173 us
  Pallas kernels  167 us (97%)
  local copies, waits for them, and re-layouts  5.02 us (3%)
    pallas_call x1, Pallas kernels, on_device(): pl.pallas_call(functools.partial(middle_kernel, ncol, nb, scale), out_sha...  77 us
    pallas_call x1, Pallas kernels, on_device(): pl.pallas_call(functools.partial(final_kernel, chips, ncol), out_shape=[j...  45.5 us
    pallas_call x1, Pallas kernels, on_device(): pl.pallas_call(functools.partial(gather_kernel, chips, nb), out_shape=jax...  24.2 us
    pallas_call x2, Pallas kernels, run_tiles(): pl.pallas_call(functools.partial(tile_kernel, back, group, blk, ncol), ou...  20.3 us
    unnamed x7, local copies, waits for them, and re-layouts  3.64 us

profile of v1, /device:TPU:1, one launch (start us, length us, event | category | flops | bytes accessed | tf_op | source)
XLA Modules:
  0.0 173.4 jit_solution(17782689090480282289)
XLA Ops:
  1.3 24.2 %gather.1.src = bf16[32,128,512]{2,1,0:T(8,128)(2,1)} custom-call(bf16[4,128,512]{2,1,0:T(8,128)(2,1)} %bitcast.13), custom_call_target="tpu_custom_call" | custom-call | tf_op jit(solution)/shard_map/gather/pallas_call | solution.py:527
  25.5 9.0 %tiles_fwd.1.part = bf16[16,128,512]{2,1,0:T(8,128)(2,1)} custom-call(s32[1]{0:T(128)} %bitcast.8.counts, s32[64]{0:T(128)} %bitcast.14, s32[64]{0:T(128)} %bitcast.16, bf16[64,128,128]{2,1,0:T(8,128)(2,1)} %bitcast.11, bf16[32,128,512]{2,1,0:T(8,128)(2,1)} %gather.1.src), custom_call_target="tpu_custom_call" | custom-call | tf_op jit(solution)/shard_map/tiles_fwd/pallas_call | solution.py:501
  34.6 77.0 %middle.1 = (bf16[512,512]{1,0:T(8,128)(2,1)}, bf16[16,128,512]{2,1,0:T(8,128)(2,1)}, bf16[2,4,80,512]{3,2,1,0:T(8,128)(2,1)}) custom-call(bf16[16,128,512]{2,1,0:T(8,128)(2,1)} %tiles_fwd.1.part, bf16[512,512]{1,0:T(8,128)(2,1)} %w.1, f32[1,512]{1,0:T(1,128)} %bitcast.19, bf16[512,512]{1,0:T(8,128)(2,1)} %cot.1), custom_call_target="tpu_custom_call" | custom-call | tf_op jit(solution)/shard_map/middle/pallas_call | solution.py:540
  111.6 11.3 %tiles_back.1 = bf16[32,128,512]{2,1,0:T(8,128)(2,1)} custom-call(s32[1]{0:T(128)} %bitcast.9.counts, s32[64]{0:T(128)} %bitcast.15, s32[64]{0:T(128)} %bitcast.17, bf16[64,128,128]{2,1,0:T(8,128)(2,1)} %bitcast.12, bf16[16,128,512]{2,1,0:T(8,128)(2,1)} %get-tuple-element.11.src), custom_call_target="tpu_custom_call" | custom-call | tf_op jit(solution)/shard_map/tiles_back/pallas_call | solution.py:501
  122.9 0.0 copy-start.1
  122.9 45.5 %final.1 = (bf16[512,512]{1,0:T(8,128)(2,1)}, f32[512,512]{1,0:T(8,128)}, f32[8,512]{1,0:T(8,128)}) custom-call(bf16[8,512,512]{2,1,0:T(8,128)(2,1)} %bitcast.10, bf16[2,4,80,512]{3,2,1,0:T(8,128)(2,1)} %get-tuple-element.12.wp), custom_call_target="tpu_custom_call" | custom-call | tf_op jit(solution)/shard_map/final/pallas_call | solution.py:563
  168.4 0.0 copy-start
  168.4 1.4 slice.3
  169.8 0.0 copy-done.1
  169.8 0.8 copy.16
  170.6 1.9 %copy.17 = bf16[512,512]{1,0:T(8,128)(2,1)} copy(bf16[512,512]{1,0:T(8,128)(2,1)} %get-tuple-element.21) | data formatting | bytes 1048576
  172.5 0.0 copy-done
  172.5 1.0 copy.18
Async XLA Ops:
  122.9 46.9 %copy-start.1 = (bf16[512,512]{1,0:T(8,128)(2,1)S(1)}, bf16[512,512]{1,0:T(8,128)(2,1)}, u32[]{:S(2)}) copy-start(bf16[512,512]{1,0:T(8,128)(2,1)} %get-tuple-element.20) | copy-start | bytes 1572868
  168.4 4.1 %copy-start = (f32[512,512]{1,0:T(8,128)S(1)}, f32[512,512]{1,0:T(8,128)}, u32[]{:S(2)}) copy-start(f32[512,512]{1,0:T(8,128)} %get-tuple-element.22) | copy-start | bytes 3145732

commit v2 on v1

--- a/solution.py
+++ b/solution.py
@@ -156,16 +156,22 @@
 
 
 def middle_kernel(
-    n, nb, scale, part, w, bias, cot, out, spread, wp,
-    acc_r, acc_l, agg, gp, accf, s_r, r_r, s_l, r_l, s_gr, r_gr, s_gl, r_gl,
+    n, chips, np_, scale, part, w, bias, cot, out, spread, ws,
+    acc_r, acc_l, agg, gp, accf, wp, w1, w2,
+    s_r, r_r, s_l, r_l, s_gr, r_gr, s_gl, r_gl, s_w1, r_w1, s_w2, r_w2,
 ):
     r, q = lax.axis_index("row"), lax.axis_index("col")
+    k, c = r // 2, r % 2
     last = n - 1
     right, left = (r, jnp.minimum(q + 1, last)), (r, jnp.maximum(q - 1, 0))
+    partner = (k * 2 + 1 - c, q)
     size = part.shape[1]
 
+    def dev(d):
+        return (flip(k, d) * 2 + c, q)
+
     def chain(buf, s, v, to, d, j, first=False):
-        at = d * nb + j
+        at = d * np_ + j
         return remote(
             (part if first else buf).at[at], buf.at[at], s.at[d, j], v.at[d, j], to
         )
@@ -174,33 +180,48 @@
     cp_l = functools.partial(chain, acc_l, s_l, r_l, left)
 
     def cp_g(s, v, to, d, j):
-        at = d * nb + j
+        at = d * np_ + j
         return remote(spread.at[at], spread.at[at], s.at[d, j], v.at[d, j], to)
 
     cp_gr = functools.partial(cp_g, s_gr, r_gr, right)
     cp_gl = functools.partial(cp_g, s_gl, r_gl, left)
-
-    def hop(cp, buf, mine, start, d, j):
-        @pl.when(mine)
-        def _():
-            @pl.when(start)
-            def _():
-                cp(d, j, True).start()
-
-            @pl.when(jnp.logical_not(start))
-            def _():
-                cp(d, j).wait_recv()
-                at = d * nb + j
-                buf[at] = (buf[at].astype(F32) + part[at].astype(F32)).astype(BF)
-                cp(d, j).start()
-
-    def reduce_block(j):
-        for i in range(n - 1):
-            hop(cp_r, acc_r, q < last - i, q == 0, last - i, j)
-            hop(cp_l, acc_l, q > i, q == last, i, j)
-
-    def finish_block(j):
-        at = q * nb + j
+    cp_w1 = remote(wp.at[1 - c], w1, s_w1.at[0], r_w1.at[0], partner)
+
+    def cp_w2(d):
+        return remote(w1.at[flip(k, d)], w2.at[d], s_w2.at[d], r_w2.at[d], dev(d))
+
+    def hop(cp, buf, start, d, j):
+        @pl.when(start)
+        def _():
+            cp(d, j, True).start()
+
+        @pl.when(jnp.logical_not(start))
+        def _():
+            cp(d, j).wait_recv()
+            at = d * np_ + j
+            buf[at] = (buf[at].astype(F32) + part[at].astype(F32)).astype(BF)
+            cp(d, j).start()
+
+    def live(j):
+        return jnp.logical_and(j >= 0, j < np_)
+
+    def reduce_step(t):
+        jr, jl = t - q, t - (last - q)
+
+        @pl.when(live(jr))
+        def _():
+            @pl.loop(0, last - q)
+            def _(i):
+                hop(cp_r, acc_r, q == 0, last - i, jr)
+
+        @pl.when(live(jl))
+        def _():
+            @pl.loop(0, q)
+            def _(i):
+                hop(cp_l, acc_l, q == last, i, jl)
+
+    def finish(j):
+        at = q * np_ + j
         accf[...] = part[at].astype(F32)
 
         @pl.when(q > 0)
@@ -213,7 +234,7 @@
             cp_l(q, j).wait_recv()
             accf[...] += acc_l[at].astype(F32)
 
-        rows = pl.ds(j * size, size)
+        rows = pl.ds(pl.multiple_of(j * size, size), size)
         a = accf[...].astype(BF)
         agg[rows, :] = a
         pre = jnp.dot(a, w[...], preferred_element_type=F32) + bias[...]
@@ -233,25 +254,27 @@
         def _():
             cp_gl(q, j).start()
 
-    def relay_block(j):
-        for o in range(1, n):
-            @pl.when(q >= o)
+    def relay(j, o):
+        @pl.when(jnp.logical_and(live(j), q >= o))
+        def _():
+            cp_gr(q - o, j).wait_recv()
+
+            @pl.when(q < last)
             def _():
-                cp_gr(q - o, j).wait_recv()
-
-                @pl.when(q < last)
-                def _():
-                    cp_gr(q - o, j).start()
-
-            @pl.when(q + o <= last)
+                cp_gr(q - o, j).start()
+
+        @pl.when(jnp.logical_and(live(j), q + o <= last))
+        def _():
+            cp_gl(q + o, j).wait_recv()
+
+            @pl.when(q > 0)
             def _():
-                cp_gl(q + o, j).wait_recv()
-
-                @pl.when(q > 0)
-                def _():
-                    cp_gl(q + o, j).start()
+                cp_gl(q + o, j).start()
 
     barrier = pltpu.get_barrier_semaphore()
+    peers = [partner] + [dev(d) for d in range(1, chips)]
+    for peer in peers:
+        pl.semaphore_signal(barrier, inc=1, device_id=peer, device_id_type=MESH)
 
     @pl.when(q > 0)
     def _():
@@ -261,19 +284,39 @@
     def _():
         pl.semaphore_signal(barrier, inc=1, device_id=right, device_id_type=MESH)
 
-    pl.semaphore_wait(barrier, jnp.minimum(q, 1) + jnp.minimum(last - q, 1))
-
-    for step in range(nb + 3):
-        if step < nb:
-            reduce_block(step)
-        if 0 <= step - 1 < nb:
-            finish_block(step - 1)
-        if 0 <= step - 3 < nb:
-            if step == nb + 2:
-                weight_block(n, scale, agg, gp, wp)
-            relay_block(step - 3)
-
-    for j in range(nb):
+    pl.semaphore_wait(barrier, jnp.minimum(q, 1) + jnp.minimum(last - q, 1) + len(peers))
+
+    @pl.loop(0, np_ + 2 * last)
+    def _(t):
+        reduce_step(t)
+        for o in range(1, n):
+            relay(t - last - o, o)
+
+        @pl.when(live(t - last))
+        def _():
+            finish(t - last)
+
+        @pl.when(t == np_ - 1 + last)
+        def _():
+            weight_block(chips, scale, agg, gp, wp)
+            cp_w1.start()
+
+        @pl.when(t == np_ - 1 + last + 1)
+        def _():
+            cp_w1.wait_recv()
+            for z in range(chips):
+                w1[z] = (w1[z].astype(F32) + wp[c, z].astype(F32)).astype(BF)
+            for d in range(1, chips):
+                cp_w2(d).start()
+
+    total = w1[k].astype(F32)
+    for d in range(1, chips):
+        cp_w2(d).wait_recv()
+        total = total + w2[d].astype(F32)
+    ws[...] = total.astype(BF)
+
+    @pl.loop(0, np_)
+    def _(j):
         for d in range(n):
             @pl.when(q < d)
             def _():
@@ -291,10 +334,14 @@
             def _():
                 cp_gl(d, j).wait_send()
 
-
-def weight_block(n, scale, agg, gp, wp):
+    cp_w1.wait_send()
+    for d in range(1, chips):
+        cp_w2(d).wait_send()
+
+
+def weight_block(parts, scale, agg, gp, wp):
     width = agg.shape[1]
-    rows = width // (2 * n)
+    rows = width // (2 * parts)
     total = jnp.sum(gp[...].astype(F32), axis=0, keepdims=True) * scale
     pad = jnp.broadcast_to(total, (PAD, width)).astype(BF)
     step = 128
@@ -308,8 +355,8 @@
         res = (res * scale).astype(BF)
         for u in range(step // rows):
             p = (t * step) // rows + u
-            wp[p // n, p % n, :rows, :] = res[u * rows : (u + 1) * rows]
-            wp[p // n, p % n, rows:, :] = pad
+            wp[p // parts, p % parts, :rows, :] = res[u * rows : (u + 1) * rows]
+            wp[p // parts, p % parts, rows:, :] = pad
 
 
 def add_rows(dst, srcs, begin, count):
@@ -325,8 +372,8 @@
 
 
 def final_kernel(
-    chips, n, part, wp, fg, wg, bg, a_buf, b_buf, c_buf, w1, w2, w3, w4,
-    s_a, r_a, s_b, r_b, s_c, r_c, s_w1, r_w1, s_w2, r_w2, s_w3, r_w3, s_w4, r_w4, s_w5, r_w5,
+    chips, n, part, ws, fg, w4, a_buf, b_buf, c_buf, w3,
+    s_a, r_a, s_b, r_b, s_c, r_c, s_w3, r_w3, s_w4, r_w4, s_w5, r_w5,
 ):
     r, q = lax.axis_index("row"), lax.axis_index("col")
     k, c = r // 2, r % 2
@@ -359,28 +406,24 @@
             a_buf.at[3, pl.ds(h * half, half)], c_buf.at[h], s_c.at[h], r_c.at[h], dev(h + 1)
         )
 
-    cp_w1 = remote(wp.at[1 - c], w1, s_w1.at[0], r_w1.at[0], partner)
-
-    def cp_w2(dz):
-        return remote(w1.at[(q + dz) % n], w2.at[dz], s_w2.at[dz], r_w2.at[dz], deep(dz))
-
-    def cp_w3(d):
-        return remote(w3.at[k], w3.at[k], s_w3.at[d], r_w3.at[d], dev(d))
-
-    def cp_w4(dz):
-        return remote(w4.at[c, q], w4.at[c, q], s_w4.at[dz], r_w4.at[dz], deep(dz))
-
-    def cp_w5(dz):
-        at = (q + n - dz) % n
-        return remote(w4.at[c, at], w4.at[c, at], s_w5.at[dz], r_w5.at[dz], partner)
+    def cp_w3(dz):
+        return remote(ws, w3.at[q], s_w3.at[dz], r_w3.at[dz], deep(dz))
+
+    def cp_w4(d):
+        return remote(w4.at[c, k], w4.at[c, k], s_w4.at[d], r_w4.at[d], dev(d))
+
+    def cp_w5(d):
+        at = flip(k, d)
+        return remote(w4.at[c, at], w4.at[c, at], s_w5.at[d], r_w5.at[d], partner)
 
     greet([partner] + [dev(d) for d in range(1, chips)] + [deep(dz) for dz in range(1, n)])
-    cp_w1.start()
     order = list(range(chips - 1, 0, -1)) + [0]
     if relay:
         order = [3, 1, 2, 0]
     for d in order:
         cp_a(d).start()
+    for dz in range(1, n):
+        cp_w3(dz).start()
 
     def join(d):
         cp_a(d).wait_recv()
@@ -400,73 +443,46 @@
             for h in range(2):
                 cp_b(d, h).start()
 
-    cp_w1.wait_recv()
-    for z in range(n):
-        w1[z] = (w1[z].astype(F32) + wp[c, z].astype(F32)).astype(BF)
+    w3[q] = ws[...]
     for dz in range(1, n):
-        cp_w2(dz).start()
+        at = (q + n - dz) % n
+        remote(w3.at[at], w3.at[at], s_w3.at[dz], r_w3.at[dz], deep(dz)).wait_recv()
+    total = w3[0].astype(F32)
+    for i in range(1, n):
+        total = total + w3[i].astype(F32)
+    w4[c, k] = total.astype(BF)
+    for d in range(1, chips):
+        cp_w4(d).start()
+    cp_w5(0).start()
 
     if relay:
         cp_c(0).wait_recv()
         add_rows(a_buf.at[2], [a_buf.at[2], c_buf.at[0]], 0, half)
         cp_b(2, 0).start()
         cp_c(1).wait_recv()
-
-        @pl.loop(0, half // 64)
-        def _(i):
-            at = pl.ds(pl.multiple_of(half + i * 64, 64), 64)
-            lo = pl.ds(pl.multiple_of(i * 64, 64), 64)
-            a_buf[1, at, :] = (
-                a_buf[1, at, :].astype(F32) + c_buf[1, lo, :].astype(F32)
-            ).astype(BF)
-
+        at = pl.ds(half, half)
+        add_rows(a_buf.at[1, at], [a_buf.at[1, at], c_buf.at[1]], 0, half)
         cp_b(1, 1).start()
 
-    total = w1[q].astype(F32)
-    for dz in range(1, n):
-        cp_w2(dz).wait_recv()
-        total = total + w2[dz].astype(F32)
-    w3[k] = total.astype(BF)
+    join(0)
     for d in range(1, chips):
-        cp_w3(d).start()
-    cp_a(0).wait_recv()
-    for d in range(1, chips):
-        other = flip(k, d)
-        remote(w3.at[other], w3.at[other], s_w3.at[d], r_w3.at[d], dev(d)).wait_recv()
-    total = w3[0].astype(F32)
-    for i in range(1, chips):
-        total = total + w3[i].astype(F32)
-    w4[c, q] = total.astype(BF)
-    for dz in range(1, n):
-        cp_w4(dz).start()
-    cp_w5(0).start()
-    for dz in range(1, n):
-        at = (q + n - dz) % n
+        at = flip(k, d)
+        remote(w4.at[c, at], w4.at[c, at], s_w4.at[d], r_w4.at[d], dev(d)).wait_recv()
+        cp_w5(d).start()
+    for h in range(2):
+        for d in near:
+            cp_b(d, (h + (d == 2)) % 2).wait_recv()
+    add_rows(fg, [a_buf.at[0]] + [b_buf.at[d] for d in near], 0, rows)
+
+    for d in range(chips):
+        at = flip(k, d)
         remote(
-            w4.at[c, at], w4.at[c, at], s_w4.at[dz], r_w4.at[dz], deep(dz)
+            w4.at[1 - c, at], w4.at[1 - c, at], s_w5.at[d], r_w5.at[d], partner
         ).wait_recv()
-        cp_w5(dz).start()
-
-    for d in near:
-        for h in range(2):
-            cp_b(d, h).wait_recv()
-    add_rows(fg, [a_buf.at[0], mine(0)] + [b_buf.at[d] for d in near], 0, rows)
-
-    for dz in range(n):
-        at = (q + n - dz) % n
-        remote(
-            w4.at[1 - c, at], w4.at[1 - c, at], s_w5.at[dz], r_w5.at[dz], partner
-        ).wait_recv()
-    take = w4.shape[2] - PAD
-    for i in range(2):
-        for z in range(n):
-            p = i * n + z
-            wg[p * take : (p + 1) * take, :] = w4[i, z, :take, :].astype(F32)
-    bg[...] = w4[0, 0, take:, :].astype(F32)[:8]
-
-    cp_w1.wait_send()
+
     for d in range(chips):
         cp_a(d).wait_send()
+        cp_w5(d).wait_send()
     for d in near:
         for h in range(2):
             cp_b(d, h).wait_send()
@@ -474,12 +490,9 @@
         for h in range(2):
             cp_c(h).wait_send()
     for d in range(1, chips):
-        cp_w3(d).wait_send()
-    for dz in range(n):
-        if dz:
-            cp_w2(dz).wait_send()
-            cp_w4(dz).wait_send()
-        cp_w5(dz).wait_send()
+        cp_w4(d).wait_send()
+    for dz in range(1, n):
+        cp_w3(dz).wait_send()
 
 
 VM = pl.BlockSpec(memory_space=pltpu.VMEM)
@@ -536,55 +549,61 @@
 
     partial = run_tiles(False, 4, nb, ncol, ncol * nb, counts, rows, cols, values, gathered)
 
-    pr = width // (2 * ncol) + PAD
-    out, spread, wp = pl.pallas_call(
-        functools.partial(middle_kernel, ncol, nb, scale),
+    part_rows = width // (2 * chips)
+    pr = part_rows + PAD
+    piece = size // 2
+    pieces = node_dev // piece
+    wide = (ncol * pieces, piece, width)
+    out, spread, ws = pl.pallas_call(
+        functools.partial(middle_kernel, ncol, chips, pieces, scale),
         out_shape=[
             jax.ShapeDtypeStruct((node_dev, width), BF),
-            jax.ShapeDtypeStruct((ncol * nb, size, width), BF),
-            jax.ShapeDtypeStruct((2, ncol, pr, width), BF),
+            jax.ShapeDtypeStruct(wide, BF),
+            jax.ShapeDtypeStruct((pr, width), BF),
         ],
         in_specs=[VM] * 4,
         out_specs=[VM] * 3,
         scratch_shapes=[
-            pltpu.VMEM((ncol * nb, size, width), BF),
-            pltpu.VMEM((ncol * nb, size, width), BF),
+            pltpu.VMEM(wide, BF),
+            pltpu.VMEM(wide, BF),
             pltpu.VMEM((node_dev, width), BF),
             pltpu.VMEM((node_dev, width), BF),
-            pltpu.VMEM((size, width), F32),
+            pltpu.VMEM((piece, width), F32),
+            pltpu.VMEM((2, chips, pr, width), BF),
+            pltpu.VMEM((chips, pr, width), BF),
+            pltpu.VMEM((chips, pr, width), BF),
         ]
-        + [dma(ncol, nb)] * 8,
+        + [dma(ncol, pieces)] * 8
+        + [dma(1), dma(1), dma(chips), dma(chips)],
         compiler_params=params(1),
         name="middle",
-    )(partial, weight, bias.reshape(1, width), cotangent)
+    )(partial.reshape(wide), weight, bias.reshape(1, width), cotangent)
+    spread = spread.reshape(ncol * nb, size, width)
 
     grads = run_tiles(True, 2, nb, ncol, nrow * nb, counts, rows, cols, values, spread)
 
-    fg, wg, bg = pl.pallas_call(
+    fg, parts = pl.pallas_call(
         functools.partial(final_kernel, chips, ncol),
         out_shape=[
             jax.ShapeDtypeStruct((node_dev, width), BF),
-            jax.ShapeDtypeStruct((width, width), F32),
-            jax.ShapeDtypeStruct((8, width), F32),
+            jax.ShapeDtypeStruct((2, chips, pr, width), BF),
         ],
         in_specs=[VM] * 2,
-        out_specs=[VM] * 3,
+        out_specs=[VM] * 2,
         scratch_shapes=[
             pltpu.VMEM((chips, node_dev, width), BF),
             pltpu.VMEM((chips, node_dev, width), BF),
             pltpu.VMEM((2, node_dev // 2, width), BF),
             pltpu.VMEM((ncol, pr, width), BF),
-            pltpu.VMEM((ncol, pr, width), BF),
-            pltpu.VMEM((chips, pr, width), BF),
-            pltpu.VMEM((2, ncol, pr, width), BF),
             dma(chips), dma(chips), dma(chips, 2), dma(chips, 2), dma(2), dma(2),
-            dma(1), dma(1), dma(ncol), dma(ncol), dma(chips), dma(chips),
-            dma(ncol), dma(ncol), dma(ncol), dma(ncol),
+            dma(ncol), dma(ncol), dma(chips), dma(chips), dma(chips), dma(chips),
         ],
         compiler_params=params(2),
         name="final",
-    )(grads.reshape(nrow, node_dev, width), wp)
-    return (out, fg, wg, bg[0])
+    )(grads.reshape(nrow, node_dev, width), ws)
+    wg = parts[:, :, :part_rows].astype(F32).reshape(width, width)
+    bg = parts[0, 0, part_rows].astype(F32)
+    return (out, fg, wg, bg)
 
 
 def solution(mesh):

time: 173 us -> 156 us (0.902)
  Pallas kernels: 167 us -> 150 us
  other arithmetic: 0 us -> 2.5 us
  local copies, waits for them, and re-layouts: 5.02 us -> 2.67 us
    pallas_call x1, Pallas kernels: 45.5 us -> 36.3 us  [on_device(): pl.pallas_call(functools.partial(final_kernel, chips, ncol), out_shape=[j...]
    pallas_call x1, Pallas kernels: 77 us -> 70.3 us  [on_device(): pl.pallas_call(functools.partial(middle_kernel, ncol, chips, pieces, scal...]
    unnamed x7 -> x6, local copies, waits for them, and re-layouts: 3.64 us -> 1.59 us
where the time goes in v2:
time: 156 us; the launch traced here: 157 us
  Pallas kernels  150 us (96%)
  local copies, waits for them, and re-layouts  2.67 us (2%)
  other arithmetic  2.5 us (2%)
    pallas_call x1, Pallas kernels, on_device(): pl.pallas_call(functools.partial(middle_kernel, ncol, chips, pieces, scal...  70.3 us
    pallas_call x1, Pallas kernels, on_device(): pl.pallas_call(functools.partial(final_kernel, chips, ncol), out_shape=[j...  36.3 us
    pallas_call x1, Pallas kernels, on_device(): pl.pallas_call(functools.partial(gather_kernel, chips, nb), out_shape=jax...  24.2 us
    pallas_call x2, Pallas kernels, run_tiles(): pl.pallas_call(functools.partial(tile_kernel, back, group, blk, ncol), ou...  19.4 us

profile of v2, /device:TPU:1, one launch (start us, length us, event | category | flops | bytes accessed | tf_op | source)
XLA Modules:
  0.0 156.7 jit_solution(12810001666165027227)
XLA Ops:
  1.3 24.2 %gather.1.src = bf16[32,128,512]{2,1,0:T(8,128)(2,1)} custom-call(bf16[4,128,512]{2,1,0:T(8,128)(2,1)} %bitcast.20), custom_call_target="tpu_custom_call" | custom-call | tf_op jit(solution)/shard_map/gather/pallas_call | solution.py:540
  25.5 9.0 %tiles_fwd.1 = bf16[16,128,512]{2,1,0:T(8,128)(2,1)} custom-call(s32[1]{0:T(128)} %bitcast.13.counts, s32[64]{0:T(128)} %bitcast.21, s32[64]{0:T(128)} %bitcast.23, bf16[64,128,128]{2,1,0:T(8,128)(2,1)} %bitcast.16, bf16[32,128,512]{2,1,0:T(8,128)(2,1)} %gather.1.src), custom_call_target="tpu_custom_call" | custom-call | tf_op jit(solution)/shard_map/tiles_fwd/pallas_call | solution.py:514
  34.6 70.3 %middle.1 = (bf16[512,512]{1,0:T(8,128)(2,1)}, bf16[32,64,512]{2,1,0:T(8,128)(2,1)}, bf16[80,512]{1,0:T(8,128)(2,1)}) custom-call(bf16[32,64,512]{2,1,0:T(8,128)(2,1)} %bitcast.18, bf16[512,512]{1,0:T(8,128)(2,1)} %w.1, f32[1,512]{1,0:T(1,128)} %bitcast.26, bf16[512,512]{1,0:T(8,128)(2,1)} %cot.1), custom_call_target="tpu_custom_call" | custom-call | tf_op jit(solution)/shard_map/middle/pallas_call | solution.py:557
  104.8 10.4 %tiles_back.1 = bf16[32,128,512]{2,1,0:T(8,128)(2,1)} custom-call(s32[1]{0:T(128)} %bitcast.14.counts, s32[64]{0:T(128)} %bitcast.22, s32[64]{0:T(128)} %bitcast.24, bf16[64,128,128]{2,1,0:T(8,128)(2,1)} %bitcast.17, bf16[16,128,512]{2,1,0:T(8,128)(2,1)} %bitcast.19), custom_call_target="tpu_custom_call" | custom-call | tf_op jit(solution)/shard_map/tiles_back/pallas_call | solution.py:514
  115.2 36.3 %final.1 = (bf16[512,512]{1,0:T(8,128)(2,1)}, bf16[2,4,80,512]{3,2,1,0:T(8,128)(2,1)}) custom-call(bf16[8,512,512]{2,1,0:T(8,128)(2,1)} %bitcast.15, bf16[80,512]{1,0:T(8,128)(2,1)} %get-tuple-element.11.ws), custom_call_target="tpu_custom_call" | custom-call | tf_op jit(solution)/shard_map/final/pallas_call | solution.py:585
  151.5 0.0 copy-start
  151.5 0.0 copy-start.1
  151.5 1.4 slice_convert_fusion
  152.9 1.1 slice.6
  154.0 1.1 bitcast_convert_fusion
  155.1 0.0 copy-done
  155.1 0.8 copy.15
  155.9 0.0 copy-done.1
  155.9 0.8 copy.16
Async XLA Ops:
  151.5 3.6 %copy-start = (bf16[512,512]{1,0:T(8,128)(2,1)S(1)}, bf16[512,512]{1,0:T(8,128)(2,1)}, u32[]{:S(2)}) copy-start(bf16[512,512]{1,0:T(8,128)(2,1)} %get-tuple-element.18) | copy-start | bytes 1572868
  151.5 4.4 %copy-start.1 = (bf16[512,512]{1,0:T(8,128)(2,1)S(1)}, bf16[512,512]{1,0:T(8,128)(2,1)}, u32[]{:S(2)}) copy-start(bf16[512,512]{1,0:T(8,128)(2,1)} %get-tuple-element.19) | copy-start | bytes 1572868

commit v3 on v2

--- a/solution.py
+++ b/solution.py
@@ -12,6 +12,7 @@
 BF = jnp.bfloat16
 F32 = jnp.float32
 PAD = 16
+WAYS = 2
 
 
 def flip(k, bits):
@@ -133,26 +134,34 @@
         lists[d * slots + n] = k
         lens[d] = n + 1
 
-    @pl.loop(0, dests)
-    def _(d):
-        m = lens[d]
-        acc[...] = jnp.zeros_like(acc)
-
-        @pl.loop(0, (m + group - 1) // group)
+    def product(d, m, t):
+        left, right = [], []
+        for i in range(group):
+            at = t * group + i
+            k = jnp.where(at < m, lists[d * slots + jnp.minimum(at, slots - 1)], 0)
+            mat = tiles[k]
+            left.append(jnp.where(at < m, mat, jnp.zeros_like(mat)))
+            right.append(src[src_of(k)])
+        lhs = jnp.concatenate(left, axis=0 if back else 1)
+        rhs = jnp.concatenate(right, axis=0)
+        dims = (((0,), (0,)), ((), ())) if back else (((1,), (0,)), ((), ()))
+        return lax.dot_general(lhs, rhs, dims, preferred_element_type=F32)
+
+    @pl.loop(0, dests // WAYS)
+    def _(e):
+        ids = [e * WAYS + i for i in range(WAYS)]
+        sizes = [lens[d] for d in ids]
+        most = functools.reduce(jnp.maximum, sizes)
+        for i in range(WAYS):
+            acc[i] = product(ids[i], sizes[i], 0)
+
+        @pl.loop(1, (most + group - 1) // group)
         def _(t):
-            left, right = [], []
-            for i in range(group):
-                at = t * group + i
-                k = lists[d * slots + jnp.minimum(at, m - 1)]
-                mat = tiles[k]
-                left.append(jnp.where(at < m, mat, jnp.zeros_like(mat)))
-                right.append(src[src_of(k)])
-            lhs = jnp.concatenate(left, axis=0 if back else 1)
-            rhs = jnp.concatenate(right, axis=0)
-            dims = (((0,), (0,)), ((), ())) if back else (((1,), (0,)), ((), ()))
-            acc[...] += lax.dot_general(lhs, rhs, dims, preferred_element_type=F32)
-
-        out[d] = acc[...].astype(BF)
+            for i in range(WAYS):
+                acc[i] = acc[i] + product(ids[i], sizes[i], t)
+
+        for i in range(WAYS):
+            out[ids[i]] = acc[i].astype(BF)
 
 
 def middle_kernel(
@@ -372,7 +381,7 @@
 
 
 def final_kernel(
-    chips, n, part, ws, fg, w4, a_buf, b_buf, c_buf, w3,
+    chips, n, part, ws, fg, w4, bg, a_buf, b_buf, c_buf, w3,
     s_a, r_a, s_b, r_b, s_c, r_c, s_w3, r_w3, s_w4, r_w4, s_w5, r_w5,
 ):
     r, q = lax.axis_index("row"), lax.axis_index("col")
@@ -480,6 +489,7 @@
             w4.at[1 - c, at], w4.at[1 - c, at], s_w5.at[d], r_w5.at[d], partner
         ).wait_recv()
 
+    bg[...] = w4[0, 0, w4.shape[2] - PAD :, :].astype(F32)[:1]
     for d in range(chips):
         cp_a(d).wait_send()
         cp_w5(d).wait_send()
@@ -519,7 +529,7 @@
         scratch_shapes=[
             pltpu.SMEM((dests * slots,), jnp.int32),
             pltpu.SMEM((dests,), jnp.int32),
-            pltpu.VMEM((size, width), F32),
+            pltpu.VMEM((WAYS, size, width), F32),
         ],
         name="tiles_back" if back else "tiles_fwd",
     )(counts, rows, cols, values, src)
@@ -551,7 +561,7 @@
 
     part_rows = width // (2 * chips)
     pr = part_rows + PAD
-    piece = size // 2
+    piece = size // 4
     pieces = node_dev // piece
     wide = (ncol * pieces, piece, width)
     out, spread, ws = pl.pallas_call(
@@ -582,14 +592,15 @@
 
     grads = run_tiles(True, 2, nb, ncol, nrow * nb, counts, rows, cols, values, spread)
 
-    fg, parts = pl.pallas_call(
+    fg, parts, bg = pl.pallas_call(
         functools.partial(final_kernel, chips, ncol),
         out_shape=[
             jax.ShapeDtypeStruct((node_dev, width), BF),
             jax.ShapeDtypeStruct((2, chips, pr, width), BF),
+            jax.ShapeDtypeStruct((1, width), F32),
         ],
         in_specs=[VM] * 2,
-        out_specs=[VM] * 2,
+        out_specs=[VM] * 3,
         scratch_shapes=[
             pltpu.VMEM((chips, node_dev, width), BF),
             pltpu.VMEM((chips, node_dev, width), BF),
@@ -602,8 +613,7 @@
         name="final",
     )(grads.reshape(nrow, node_dev, width), ws)
     wg = parts[:, :, :part_rows].astype(F32).reshape(width, width)
-    bg = parts[0, 0, part_rows].astype(F32)
-    return (out, fg, wg, bg)
+    return (out, fg, wg, bg.reshape(width))
 
 
 def solution(mesh):

time: 156 us -> 165 us (1.058)
  Pallas kernels: 150 us -> 159 us
    pallas_call x1, Pallas kernels: 70.3 us -> 85.5 us  [on_device(): pl.pallas_call(functools.partial(middle_kernel, ncol, chips, pieces, scal...]
    pallas_call x1, Pallas kernels: 36.3 us -> 31.7 us  [on_device(): pl.pallas_call(functools.partial(final_kernel, chips, ncol), out_shape=[j...]
where the time goes in v3:
time: 165 us
  Pallas kernels  159 us (96%)
  local copies, waits for them, and re-layouts  3.34 us (2%)
    pallas_call x1, Pallas kernels, on_device(): pl.pallas_call(functools.partial(middle_kernel, ncol, chips, pieces, scal...  85.5 us
    pallas_call x1, Pallas kernels, on_device(): pl.pallas_call(functools.partial(final_kernel, chips, ncol), out_shape=[j...  31.7 us
    pallas_call x1, Pallas kernels, on_device(): pl.pallas_call(functools.partial(gather_kernel, chips, nb), out_shape=jax...  24.2 us
    pallas_call x2, Pallas kernels, run_tiles(): pl.pallas_call(functools.partial(tile_kernel, back, group, blk, ncol), ou...  17.8 us

profile of v3, /device:TPU:1, one launch (start us, length us, event | category | flops | bytes accessed | tf_op | source)
XLA Modules:
  0.0 165.1 jit_solution(4796082188943484356)
XLA Ops:
  1.3 24.2 %gather.1.src = bf16[32,128,512]{2,1,0:T(8,128)(2,1)} custom-call(bf16[4,128,512]{2,1,0:T(8,128)(2,1)} %bitcast.20), custom_call_target="tpu_custom_call" | custom-call | tf_op jit(solution)/shard_map/gather/pallas_call | solution.py:550
  25.5 7.6 %tiles_fwd.1 = bf16[16,128,512]{2,1,0:T(8,128)(2,1)} custom-call(s32[1]{0:T(128)} %bitcast.13.counts, s32[64]{0:T(128)} %bitcast.21, s32[64]{0:T(128)} %bitcast.23, bf16[64,128,128]{2,1,0:T(8,128)(2,1)} %bitcast.16, bf16[32,128,512]{2,1,0:T(8,128)(2,1)} %gather.1.src), custom_call_target="tpu_custom_call" | custom-call | tf_op jit(solution)/shard_map/tiles_fwd/pallas_call | solution.py:524
  33.1 85.5 %middle.1 = (bf16[512,512]{1,0:T(8,128)(2,1)}, bf16[64,32,512]{2,1,0:T(8,128)(2,1)}, bf16[80,512]{1,0:T(8,128)(2,1)}) custom-call(bf16[64,32,512]{2,1,0:T(8,128)(2,1)} %bitcast.18, bf16[512,512]{1,0:T(8,128)(2,1)} %w.1, f32[1,512]{1,0:T(1,128)} %bitcast.26, bf16[512,512]{1,0:T(8,128)(2,1)} %cot.1), custom_call_target="tpu_custom_call" | custom-call | tf_op jit(solution)/shard_map/middle/pallas_call | solution.py:567
  118.6 10.2 %tiles_back.1 = bf16[32,128,512]{2,1,0:T(8,128)(2,1)} custom-call(s32[1]{0:T(128)} %bitcast.14.counts, s32[64]{0:T(128)} %bitcast.22, s32[64]{0:T(128)} %bitcast.24, bf16[64,128,128]{2,1,0:T(8,128)(2,1)} %bitcast.17, bf16[16,128,512]{2,1,0:T(8,128)(2,1)} %bitcast.19), custom_call_target="tpu_custom_call" | custom-call | tf_op jit(solution)/shard_map/tiles_back/pallas_call | solution.py:524
  128.8 31.7 %final.1 = (bf16[512,512]{1,0:T(8,128)(2,1)}, bf16[2,4,80,512]{3,2,1,0:T(8,128)(2,1)}, f32[1,512]{1,0:T(1,128)}) custom-call(bf16[8,512,512]{2,1,0:T(8,128)(2,1)} %bitcast.15, bf16[80,512]{1,0:T(8,128)(2,1)} %get-tuple-element.12.ws), custom_call_target="tpu_custom_call" | custom-call | tf_op jit(solution)/shard_map/final/pallas_call | solution.py:595
  160.6 0.0 copy-start
  160.6 0.0 copy-start.1
  160.6 1.2 slice.3
  161.7 0.0 copy-start.2
  161.8 1.1 bitcast_convert_fusion
  162.9 0.0 copy-done
  162.9 0.8 copy.16
  163.7 0.0 copy-done.1
  163.7 0.8 copy.17
  164.5 0.0 copy-done.2
  164.5 0.6 copy.18
Async XLA Ops:
  160.6 2.3 %copy-start = (bf16[512,512]{1,0:T(8,128)(2,1)S(1)}, bf16[512,512]{1,0:T(8,128)(2,1)}, u32[]{:S(2)}) copy-start(bf16[512,512]{1,0:T(8,128)(2,1)} %get-tuple-element.20) | copy-start | bytes 1572868
  160.6 3.1 %copy-start.1 = (bf16[512,512]{1,0:T(8,128)(2,1)S(1)}, bf16[512,512]{1,0:T(8,128)(2,1)}, u32[]{:S(2)}) copy-start(bf16[512,512]{1,0:T(8,128)(2,1)} %get-tuple-element.21) | copy-start | bytes 1572868
  161.7 2.7 %copy-start.2 = (f32[1,512]{1,0:T(1,128)S(1)}, f32[1,512]{1,0:T(1,128)}, u32[]{:S(2)}) copy-start(f32[1,512]{1,0:T(1,128)} %get-tuple-element.15) | copy-start | bytes 6148

commit v4 on v3

--- a/solution.py
+++ b/solution.py
@@ -561,7 +561,7 @@
 
     part_rows = width // (2 * chips)
     pr = part_rows + PAD
-    piece = size // 4
+    piece = size // 2
     pieces = node_dev // piece
     wide = (ncol * pieces, piece, width)
     out, spread, ws = pl.pallas_call(

time: 165 us -> 151 us (0.915)
  Pallas kernels: 159 us -> 145 us
    pallas_call x1, Pallas kernels: 85.5 us -> 70.5 us  [on_device(): pl.pallas_call(functools.partial(middle_kernel, ncol, chips, pieces, scal...]
where the time goes in v4:
time: 151 us
  Pallas kernels  145 us (96%)
  local copies, waits for them, and re-layouts  3.34 us (2%)
    pallas_call x1, Pallas kernels, on_device(): pl.pallas_call(functools.partial(middle_kernel, ncol, chips, pieces, scal...  70.5 us
    pallas_call x1, Pallas kernels, on_device(): pl.pallas_call(functools.partial(final_kernel, chips, ncol), out_shape=[j...  32.6 us
    pallas_call x1, Pallas kernels, on_device(): pl.pallas_call(functools.partial(gather_kernel, chips, nb), out_shape=jax...  24.2 us
    pallas_call x2, Pallas kernels, run_tiles(): pl.pallas_call(functools.partial(tile_kernel, back, group, blk, ncol), ou...  18 us

profile of v4, /device:TPU:1, one launch (start us, length us, event | category | flops | bytes accessed | tf_op | source)
XLA Modules:
  0.0 151.2 jit_solution(12573180850950174644)
XLA Ops:
  1.3 24.2 %gather.1.src = bf16[32,128,512]{2,1,0:T(8,128)(2,1)} custom-call(bf16[4,128,512]{2,1,0:T(8,128)(2,1)} %bitcast.20), custom_call_target="tpu_custom_call" | custom-call | tf_op jit(solution)/shard_map/gather/pallas_call | solution.py:550
  25.5 7.8 %tiles_fwd.1 = bf16[16,128,512]{2,1,0:T(8,128)(2,1)} custom-call(s32[1]{0:T(128)} %bitcast.13.counts, s32[64]{0:T(128)} %bitcast.21, s32[64]{0:T(128)} %bitcast.23, bf16[64,128,128]{2,1,0:T(8,128)(2,1)} %bitcast.16, bf16[32,128,512]{2,1,0:T(8,128)(2,1)} %gather.1.src), custom_call_target="tpu_custom_call" | custom-call | tf_op jit(solution)/shard_map/tiles_fwd/pallas_call | solution.py:524
  33.3 70.5 %middle.1 = (bf16[512,512]{1,0:T(8,128)(2,1)}, bf16[32,64,512]{2,1,0:T(8,128)(2,1)}, bf16[80,512]{1,0:T(8,128)(2,1)}) custom-call(bf16[32,64,512]{2,1,0:T(8,128)(2,1)} %bitcast.18, bf16[512,512]{1,0:T(8,128)(2,1)} %w.1, f32[1,512]{1,0:T(1,128)} %bitcast.26, bf16[512,512]{1,0:T(8,128)(2,1)} %cot.1), custom_call_target="tpu_custom_call" | custom-call | tf_op jit(solution)/shard_map/middle/pallas_call | solution.py:567
  103.8 10.2 %tiles_back.1 = bf16[32,128,512]{2,1,0:T(8,128)(2,1)} custom-call(s32[1]{0:T(128)} %bitcast.14.counts, s32[64]{0:T(128)} %bitcast.22, s32[64]{0:T(128)} %bitcast.24, bf16[64,128,128]{2,1,0:T(8,128)(2,1)} %bitcast.17, bf16[16,128,512]{2,1,0:T(8,128)(2,1)} %bitcast.19), custom_call_target="tpu_custom_call" | custom-call | tf_op jit(solution)/shard_map/tiles_back/pallas_call | solution.py:524
  114.1 32.6 %final.1 = (bf16[512,512]{1,0:T(8,128)(2,1)}, bf16[2,4,80,512]{3,2,1,0:T(8,128)(2,1)}, f32[1,512]{1,0:T(1,128)}) custom-call(bf16[8,512,512]{2,1,0:T(8,128)(2,1)} %bitcast.15, bf16[80,512]{1,0:T(8,128)(2,1)} %get-tuple-element.12.ws), custom_call_target="tpu_custom_call" | custom-call | tf_op jit(solution)/shard_map/final/pallas_call | solution.py:595
  146.7 0.0 copy-start
  146.7 0.0 copy-start.1
  146.7 1.2 slice.3
  147.9 0.0 copy-start.2
  147.9 1.1 bitcast_convert_fusion
  149.0 0.0 copy-done
  149.0 0.8 copy.16
  149.8 0.0 copy-done.1
  149.8 0.8 copy.17
  150.6 0.0 copy-done.2
  150.6 0.6 copy.18
Async XLA Ops:
  146.7 2.3 %copy-start = (bf16[512,512]{1,0:T(8,128)(2,1)S(1)}, bf16[512,512]{1,0:T(8,128)(2,1)}, u32[]{:S(2)}) copy-start(bf16[512,512]{1,0:T(8,128)(2,1)} %get-tuple-element.20) | copy-start | bytes 1572868
  146.7 3.1 %copy-start.1 = (bf16[512,512]{1,0:T(8,128)(2,1)S(1)}, bf16[512,512]{1,0:T(8,128)(2,1)}, u32[]{:S(2)}) copy-start(bf16[512,512]{1,0:T(8,128)(2,1)} %get-tuple-element.21) | copy-start | bytes 1572868
  147.9 2.7 %copy-start.2 = (f32[1,512]{1,0:T(1,128)S(1)}, f32[1,512]{1,0:T(1,128)}, u32[]{:S(2)}) copy-start(f32[1,512]{1,0:T(1,128)} %get-tuple-element.15) | copy-start | bytes 6148
